TPU v7x, 32 devices: a whole 2x2x4 slice. The times are simulated.
32 devices in a mesh: slab: 8 (over z, y), grp: 4 (over x, core).
Axes of the slice: x: 2, y: 2, z: 4, core: 2. Of those that a mesh axis runs over, the one named last changes fastest.
Arguments:
- potential: bfloat16 [64, 8, 1024], P('slab'), may hold values from -3 to 3
- coefficients: bfloat16 [128, 16, 8, 1024], P(('slab', 'grp')), may hold values from -1 to 1
- box_center: int32 [128], replicated, may hold values from 0 to 63, as said below
- box_extent: int32 [128], replicated, may hold values from 8 to 16
Outputs:
- margin: float32 [128, 80], P(('slab', 'grp'))
- hamiltonian: float32 [128, 80], P(('slab', 'grp'))
Inputs may be any that keep to these rules, and one draw needn't show every extreme that they name: `box_center`: function b's centre lies among the 8 planes of slab b // 16, that is from (8 * (b // 16)) on.
All inputs are finite; a program needn't handle non-finite values.
Results may differ from a plain program's by a relative error of at most 0.0003.
Values may be sent and summed in bfloat16 or wider, within the bound.
A program may use at most 64 MiB of HBM per device.

v0:
```python
import jax
import jax.numpy as jnp
from jax import lax
from jax.sharding import PartitionSpec as P

COMP = 8
CX = 32
CY = 32


def with_halo(value, sides, width):
    for axis, dim in sides:
        size, length = (lax.axis_size(axis), value.shape[dim])
        up = [(i, (i + 1) % size) for i in range(size)]
        down = [(j, i) for i, j in up]
        last = lax.slice_in_dim(value, length - width, length, axis=dim)
        initial = lax.slice_in_dim(value, 0, width, axis=dim)
        before = lax.ppermute(last, axis, up)
        after = lax.ppermute(initial, axis, down)
        value = jnp.concatenate([before, value, after], axis=dim)
    return value


def shifted(value, axis, steps):
    count = lax.axis_size(axis)
    pairs = [(source, (source + steps) % count) for source in range(count)]
    return lax.ppermute(value, axis, pairs)


def haar_signs():
    row_ids = jnp.arange(COMP, dtype=jnp.int32)[:, None]
    col_ids = jnp.arange(COMP, dtype=jnp.int32)[None, :]
    common = jnp.bitwise_and(row_ids, col_ids)
    parity = (common % 2 + common // 2 % 2 + common // 4 % 2) % 2
    return (1 - 2 * parity).astype(jnp.float32)


def laplace_plane():
    cells = jnp.arange(CX * CY, dtype=jnp.int32)
    first_x = (cells // CY)[:, None]
    second_x = (cells // CY)[None, :]
    first_y = (cells % CY)[:, None]
    second_y = (cells % CY)[None, :]
    step_x = jnp.abs(first_x - second_x)
    step_y = jnp.abs(first_y - second_y)
    beside = (step_x == 1) & (first_y == second_y) | (step_y == 1) & (first_x == second_x)
    same_cell = (first_x == second_x) & (first_y == second_y)
    return jnp.where(same_cell, 2.0, jnp.where(beside, -0.5, 0.0)).astype(jnp.bfloat16)


def apply_hamiltonian(orbital, pot_box, inside):
    cell_count = orbital.shape[3]
    plane_term = jnp.dot(
        orbital.reshape(-1, cell_count), laplace_plane(), preferred_element_type=jnp.float32
    ).reshape(orbital.shape)
    padded = jnp.pad(orbital, ((0, 0), (1, 1), (0, 0), (0, 0)))
    depth_term = orbital.astype(jnp.float32) - 0.5 * (
        padded[:, :-2].astype(jnp.float32) + padded[:, 2:].astype(jnp.float32)
    )
    haar_table = haar_signs()
    fine_values = jnp.einsum(
        "kc,npcx->npkx",
        haar_table.astype(jnp.bfloat16),
        orbital,
        preferred_element_type=jnp.float32,
    )
    potential_term = (
        jnp.einsum(
            "kc,npkx->npcx",
            haar_table,
            pot_box.astype(jnp.float32) * fine_values,
            precision=lax.Precision.HIGHEST,
        )
        / COMP
    )
    return jnp.where(inside, plane_term + depth_term + potential_term, 0.0).astype(jnp.bfloat16)


def place_planes(starts, frame_depth, tile_data):
    source = jnp.arange(tile_data.shape[1], dtype=jnp.int32)
    target = jnp.arange(frame_depth, dtype=jnp.int32)
    onehot = (starts[:, None, None] + source[None, None, :] == target[None, :, None]).astype(
        jnp.bfloat16
    )
    placed = jnp.einsum("nqp,npcx->nqcx", onehot, tile_data, preferred_element_type=jnp.float32)
    return placed.astype(jnp.bfloat16)


def into_band(block_rows, offset, members):
    return jnp.pad(block_rows, ((0, 0), (offset * members, (2 - offset) * members)))


def local(potential, coefficients, box_center, box_extent):
    slab_index = lax.axis_index("slab")
    group_index = lax.axis_index("grp")
    groups = lax.axis_size("grp")
    per_device = coefficients.shape[0]
    box_depth = coefficients.shape[1]
    slab_depth = potential.shape[0]
    rim_depth = box_depth // 2
    frame_depth = slab_depth + box_depth
    members = groups * per_device
    first_row = (slab_index * groups + group_index) * per_device
    centers = lax.dynamic_slice_in_dim(box_center, first_row, per_device)
    extents = lax.dynamic_slice_in_dim(box_extent, first_row, per_device)
    frame_starts = centers - slab_index * slab_depth - extents // 2 + rim_depth
    planes = jnp.arange(box_depth, dtype=jnp.int32)
    inside = (planes[None, :] < extents[:, None])[:, :, None, None]
    orbital = jnp.where(inside, coefficients, jnp.zeros((), jnp.bfloat16))
    pot_frame = with_halo(potential, (("slab", 0),), rim_depth)
    padded_pot = jnp.pad(pot_frame, ((0, box_depth), (0, 0), (0, 0)))

    def cut_box(start_at):
        return lax.dynamic_slice_in_dim(padded_pot, start_at, box_depth, 0)

    pot_box = jax.vmap(cut_box)(frame_starts)
    applied = apply_hamiltonian(orbital, pot_box, inside)
    frame_orbital = place_planes(frame_starts, frame_depth, orbital)
    frame_applied = place_planes(frame_starts, frame_depth, applied)
    got_orbital, got_applied = (
        lax.all_to_all(frame_orbital, "grp", split_axis=3, concat_axis=0, tiled=True),
        lax.all_to_all(frame_applied, "grp", split_axis=3, concat_axis=0, tiled=True),
    )
    middle_orbital = got_orbital[:, rim_depth : rim_depth + slab_depth]
    middle_applied = got_applied[:, rim_depth : rim_depth + slab_depth]
    lower_set = None
    upper_set = None
    for direction in (1, -1):
        if direction == 1:
            sent_orbital = got_orbital[:, rim_depth + slab_depth :]
            sent_applied = got_applied[:, rim_depth + slab_depth :]
        else:
            sent_orbital = got_orbital[:, :rim_depth]
            sent_applied = got_applied[:, :rim_depth]
        came_orbital, came_applied = shifted((sent_orbital, sent_applied), "slab", direction)
        placed_pair = (came_orbital, came_applied)
        if direction == 1:
            lower_set = placed_pair
        else:
            upper_set = placed_pair
    tile_orbital = jnp.concatenate([lower_set[0], middle_orbital, upper_set[0]], axis=0)
    tile_applied = jnp.concatenate([lower_set[1], middle_applied, upper_set[1]], axis=0)
    flat_orbital = tile_orbital.reshape(tile_orbital.shape[0], -1)
    flat_applied = tile_applied.reshape(tile_applied.shape[0], -1)
    contract = (((1,), (1,)), ((), ()))
    part_margin = lax.dot_general(
        flat_orbital, flat_orbital, contract, preferred_element_type=jnp.float32
    )
    part_ham = lax.dot_general(
        flat_applied, flat_orbital, contract, preferred_element_type=jnp.float32
    )
    total_margin = into_band(part_margin[members : 2 * members], 1, members)
    total_ham = into_band(part_ham[members : 2 * members], 1, members)
    for direction in (1, -1):
        if direction == 1:
            sent_margin = part_margin[2 * members :]
            sent_ham = part_ham[2 * members :]
        else:
            sent_margin = part_margin[:members]
            sent_ham = part_ham[:members]
        came_margin, came_ham = shifted((sent_margin, sent_ham), "slab", direction)
        offset = 0 if direction == 1 else 2
        total_margin = total_margin + into_band(came_margin, offset, members)
        total_ham = total_ham + into_band(came_ham, offset, members)
    margin, hamiltonian = (
        lax.psum_scatter(total_margin, "grp", scatter_dimension=0, tiled=True),
        lax.psum_scatter(total_ham, "grp", scatter_dimension=0, tiled=True),
    )
    return (margin, hamiltonian)


def solution(mesh):
    return jax.shard_map(
        local,
        mesh=mesh,
        in_specs=(P("slab", None, None), P(("slab", "grp"), None, None, None), P(), P()),
        out_specs=(P(("slab", "grp"), None), P(("slab", "grp"), None)),
        check_vma=False,
    )
```

profile of v0, /device:TPU:0, one launch (start us, length us, event | category | flops | bytes accessed | tf_op | source)
XLA Modules:
  0.0 191.3 jit_solution(1780533823639298639)
XLA Ops:
  0.6 3.0 %collective-permute-start.4 = (bf16[8,8,1024]{2,1,0:T(8,128)(2,1)}, bf16[8,8,1024]{2,1,0:T(8,128)(2,1)S(1)}, u32[]{:S(2)}, u32[]{:S(2)}) collective-permute-start(bf16[8,8,1024]{2,1,0:T(8,128)(2,1)} %param.4), channel_id=1, source_target_pairs={{0,4},{4,8},{8,12},{12,16},{16,20},{20,24},{24,28},{28,0},{1,5},{5... | collective-permute-start | bytes 393224 | tf_op jit(solution)/shard_map/ppermute | solution.py:18
  3.7 3.1 %collective-permute-start.5 = (bf16[8,8,1024]{2,1,0:T(8,128)(2,1)}, bf16[8,8,1024]{2,1,0:T(8,128)(2,1)S(1)}, u32[]{:S(2)}, u32[]{:S(2)}) collective-permute-start(bf16[8,8,1024]{2,1,0:T(8,128)(2,1)} %param.4), channel_id=1, source_target_pairs={{4,0},{8,4},{12,8},{16,12},{20,16},{24,20},{28,24},{0,28},{5,1},{9... | collective-permute-start | bytes 393224 | tf_op jit(solution)/shard_map/ppermute | solution.py:19
  7.7 1.4 broadcast_select_fusion
  9.1 1.0 convolution_convert_fusion.1
  10.0 12.2 %copy.11 = bf16[4,24,8,1024]{1,2,0,3:T(8,128)(2,1)} copy(bf16[4,24,8,1024]{3,1,2,0:T(8,128)(2,1)S(1)} %convolution_convert_fusion.1) | data formatting | bytes 3145728 | tf_op jit(solution)/shard_map/convert_element_type | solution.py:86
  22.2 13.3 %reshape.116 = bf16[4,2,98304]{2,1,0:T(2,128)(2,1)} reshape(bf16[1024,4,8,24]{3,2,1,0:T(8,128)(2,1)} %bitcast.55) | data formatting | bytes 3145728
  35.5 4.5 %all-to-all-start = ((bf16[4,2,98304]{2,1,0:T(2,128)(2,1)}), bf16[4,2,98304]{2,1,0:T(2,128)(2,1)}, u32[]{:S(2)}, u32[]{:S(2)}) async-start(bf16[4,2,98304]{2,1,0:T(2,128)(2,1)} %reshape.116), calls=%async_computation | async-start | bytes 3145728 | tf_op jit(solution)/shard_map/all_to_all | solution.py:121
  40.1 5.2 %fusion.2 = f32[4,16,8,1024]{3,2,1,0:T(8,128)} fusion(bf16[4,16,8,1024]{3,2,1,0:T(8,128)(2,1)S(1)} %broadcast_select_fusion, s32[1024]{0:T(1024)S(1)} %get-tuple-element.19, s32[1024]{0:T(1024)S(1)} %get-tuple-element.20), kind=kOutput, calls=%fused_computation.9 | convolution fusion | flops 1089470464 | bytes 3153920 | tf_op jit(solution)/shard_map/dot_general | solution.py:53
  46.2 0.9 fusion.31
  47.1 2.7 %gather_fusion = bf16[4,16,8,1024]{3,2,1,0:T(8,128)(2,1)} fusion(bf16[40,8,1024]{2,1,0:T(8,128)(2,1)} %fusion.31, s32[4]{0:T(128)S(1)} %get-tuple-element.4), kind=kCustom, calls=%fused_computation | custom fusion | bytes 2097200 | tf_op jit(solution)/shard_map/vmap()/gather | solution.py:114
  49.7 4.4 %fusion.5 = bf16[4,16,8,1024]{3,2,1,0:T(8,128)(2,1)S(1)} fusion(f32[4,16,8,1024]{3,2,1,0:T(8,128)} %fusion.2, bf16[4,16,8,1024]{3,2,1,0:T(8,128)(2,1)S(1)} %broadcast_select_fusion, f32[4,16,1024,8]{2,3,1,0:T(8,128)S(1)} %fusion.59, bf16[4,16,8,1024]{3,2,1,0:T(8,128)(2,1)} %gather_fusion, pred[4,16]{1,0:T(4,128)(4,1)S(1)} %iota_compare_fusion.2), kind=kOutput, calls=%fused_computation.12 | convolution fusion | flops 57151744 | bytes 7340096 | tf_op jit(solution)/shard_map/kc,npkx->npcx/dot_general | solution.py:68
  54.2 0.9 convolution_convert_fusion
  55.1 12.2 %copy.14 = bf16[4,24,8,1024]{1,2,0,3:T(8,128)(2,1)} copy(bf16[4,24,8,1024]{3,1,2,0:T(8,128)(2,1)S(1)} %convolution_convert_fusion) | data formatting | bytes 3145728 | tf_op jit(solution)/shard_map/convert_element_type | solution.py:86
  67.4 13.3 %reshape.118 = bf16[4,2,98304]{2,1,0:T(2,128)(2,1)} reshape(bf16[1024,4,8,24]{3,2,1,0:T(8,128)(2,1)} %bitcast.56) | data formatting | bytes 3145728
  80.6 3.8 %all-to-all-start.1 = ((bf16[4,2,98304]{2,1,0:T(2,128)(2,1)}), bf16[4,2,98304]{2,1,0:T(2,128)(2,1)S(1)}, u32[]{:S(2)}, u32[]{:S(2)}) async-start(bf16[4,2,98304]{2,1,0:T(2,128)(2,1)} %reshape.118), calls=%async_computation.1 | async-start | bytes 3145728 | tf_op jit(solution)/shard_map/all_to_all | solution.py:122
  84.4 14.1 %reshape.117 = bf16[1024,4,8,24]{3,2,1,0:T(8,128)(2,1)} reshape(bf16[4,2,98304]{2,1,0:T(2,128)(2,1)} %all-to-all-done) | data formatting | bytes 3145728
  98.5 12.8 %copy.12 = bf16[4,24,8,4,256]{4,0,3,2,1:T(4,128)(2,1)} copy(bf16[4,24,8,4,256]{1,2,0,4,3:T(8,128)(2,1)} %bitcast.57) | data formatting | bytes 3145728 | tf_op jit(solution)/shard_map/all_to_all | solution.py:121
  111.2 2.4 %all_to_all.29 = bf16[16,24,8,256]{3,0,2,1:T(8,128)(2,1)S(1)} reshape(bf16[4,4,24,8,256]{4,1,0,3,2:T(4,128)(2,1)} %bitcast.59) | data formatting | bytes 3145728 | tf_op jit(solution)/shard_map/all_to_all | solution.py:121
  113.6 1.2 fusion.85
  114.8 4.7 %collective-permute-start.1 = (bf16[16,8,8,256]{3,0,2,1:T(8,128)(2,1)}, bf16[16,8,8,256]{3,0,2,1:T(8,128)(2,1)}, u32[]{:S(2)}, u32[]{:S(2)}) collective-permute-start(bf16[16,8,8,256]{3,0,2,1:T(8,128)(2,1)} %get-tuple-element.11), channel_id=1, source_target_pairs={{0,28},{4,0},{8,4},{12,8},{16,12},{20,16},{24,20},{28,24},{1,29},{... | collective-permute-start | bytes 1572872 | tf_op jit(solution)/shard_map/ppermute | solution.py:27
  119.5 13.4 %reshape.119 = bf16[1024,4,8,24]{3,2,1,0:T(8,128)(2,1)} reshape(bf16[4,2,98304]{2,1,0:T(2,128)(2,1)S(1)} %all-to-all-done.1) | data formatting | bytes 3145728
  132.9 12.3 %copy.15 = bf16[4,24,8,4,256]{4,0,3,2,1:T(4,128)(2,1)S(1)} copy(bf16[4,24,8,4,256]{1,2,0,4,3:T(8,128)(2,1)} %bitcast.58) | data formatting | bytes 3145728 | tf_op jit(solution)/shard_map/all_to_all | solution.py:122
  145.7 1.0 fusion.84
  146.7 4.7 %collective-permute-start.7 = (bf16[16,8,8,256]{3,0,2,1:T(8,128)(2,1)S(1)}, bf16[16,8,8,256]{3,0,2,1:T(8,128)(2,1)S(1)}, u32[]{:S(2)}, u32[]{:S(2)}) collective-permute-start(bf16[16,8,8,256]{3,0,2,1:T(8,128)(2,1)S(1)} %get-tuple-element.8), channel_id=1, source_target_pairs={{0,28},{4,0},{8,4},{12,8},{16,12},{20,16},{24,20},{28,24},{1,29},{... | collective-permute-start | bytes 1572872 | tf_op jit(solution)/shard_map/ppermute | solution.py:27
  152.7 2.1 %convolution_bitcast_fusion = f32[48,48]{1,0:T(8,128)S(1)} fusion(bf16[16,8,8,256]{3,0,2,1:T(8,128)(2,1)} %collective-permute-done.1, bf16[16,8,8,256]{3,0,2,1:T(8,128)(2,1)S(1)} %copy-done, bf16[16,8,8,256]{3,0,2,1:T(8,128)(2,1)} %collective-permute-done), kind=kOutput, calls=%fused_computation.38 | convolution fusion | flops 80216064 | bytes 1582080 | tf_op jit(solution)/shard_map/dot_general | solution.py:146
  154.8 4.7 %collective-permute-start.3 = (f32[16,48]{1,0:T(8,128)S(1)}, f32[16,48]{1,0:T(8,128)S(1)}, u32[]{:S(2)}, u32[]{:S(2)}) collective-permute-start(f32[16,48]{1,0:T(8,128)S(1)} %get-tuple-element.17), channel_id=1, source_target_pairs={{0,28},{4,0},{8,4},{12,8},{16,12},{20,16},{24,20},{28,24},{1,29},{... | collective-permute-start | bytes 9224 | tf_op jit(solution)/shard_map/ppermute | solution.py:27
  159.6 9.9 %collective-permute-done.6 = bf16[16,8,8,256]{3,0,2,1:T(8,128)(2,1)S(1)} collective-permute-done((bf16[16,8,8,256]{3,0,2,1:T(8,128)(2,1)}, bf16[16,8,8,256]{3,0,2,1:T(8,128)(2,1)S(1)}, u32[]{:S(2)}, u32[]{:S(2)}) %collective-permute-start.6) | collective-permute-done | bytes 524320 | tf_op jit(solution)/shard_map/ppermute | solution.py:27
  169.5 2.2 %collective-permute-done.7 = bf16[16,8,8,256]{3,0,2,1:T(8,128)(2,1)S(1)} collective-permute-done((bf16[16,8,8,256]{3,0,2,1:T(8,128)(2,1)S(1)}, bf16[16,8,8,256]{3,0,2,1:T(8,128)(2,1)S(1)}, u32[]{:S(2)}, u32[]{:S(2)}) %collective-permute-start.7) | collective-permute-done | bytes 524320 | tf_op jit(solution)/shard_map/ppermute | solution.py:27
  171.7 1.8 fusion.25
  173.7 4.6 %collective-permute-start.9 = (f32[16,48]{1,0:T(8,128)S(1)}, f32[16,48]{1,0:T(8,128)S(1)}, u32[]{:S(2)}, u32[]{:S(2)}) collective-permute-start(f32[16,48]{1,0:T(8,128)S(1)} %get-tuple-element.14), channel_id=1, source_target_pairs={{0,28},{4,0},{8,4},{12,8},{16,12},{20,16},{24,20},{28,24},{1,29},{... | collective-permute-start | bytes 9224 | tf_op jit(solution)/shard_map/ppermute | solution.py:27
  178.3 1.5 collective-permute-done.8
  180.0 10.1 %all-reduce.11 = (f32[16,80]{1,0:T(8,128)S(1)}, f32[16,80]{1,0:T(8,128)S(1)}) all-reduce(f32[16,80]{1,0:T(8,128)S(1)} %pad_add_fusion.1, f32[16,80]{1,0:T(8,128)S(1)} %pad_add_fusion), channel_id=2, replica_groups=mesh['slab'=8,'grp'=4] {'grp'}, use_global_device_ids=true, to_apply=%region_0.1.clone | all-reduce | flops 2560 | bytes 20480
  (33 shorter events, 4.4 us)
Async XLA Ops:
  0.6 45.1 %collective-permute-start.4 = (bf16[8,8,1024]{2,1,0:T(8,128)(2,1)}, bf16[8,8,1024]{2,1,0:T(8,128)(2,1)S(1)}, u32[]{:S(2)}, u32[]{:S(2)}) collective-permute-start(bf16[8,8,1024]{2,1,0:T(8,128)(2,1)} %param.4), channel_id=1, source_target_pairs={{0,4},{4,8},{8,12},{12,16},{16,20},{20,24},{24,28},{28,0},{1,5},{5... | collective-permute-start | bytes 393224 | tf_op jit(solution)/shard_map/ppermute | solution.py:18
  3.7 42.1 %collective-permute-start.5 = (bf16[8,8,1024]{2,1,0:T(8,128)(2,1)}, bf16[8,8,1024]{2,1,0:T(8,128)(2,1)S(1)}, u32[]{:S(2)}, u32[]{:S(2)}) collective-permute-start(bf16[8,8,1024]{2,1,0:T(8,128)(2,1)} %param.4), channel_id=1, source_target_pairs={{4,0},{8,4},{12,8},{16,12},{20,16},{24,20},{28,24},{0,28},{5,1},{9... | collective-permute-start | bytes 393224 | tf_op jit(solution)/shard_map/ppermute | solution.py:19
  35.5 45.1 %all-to-all-start = ((bf16[4,2,98304]{2,1,0:T(2,128)(2,1)}), bf16[4,2,98304]{2,1,0:T(2,128)(2,1)}, u32[]{:S(2)}, u32[]{:S(2)}) async-start(bf16[4,2,98304]{2,1,0:T(2,128)(2,1)} %reshape.116), calls=%async_computation | async-start | bytes 3145728 | tf_op jit(solution)/shard_map/all_to_all | solution.py:121
  45.2 0.9 copy-start.1
  80.6 38.9 %all-to-all-start.1 = ((bf16[4,2,98304]{2,1,0:T(2,128)(2,1)}), bf16[4,2,98304]{2,1,0:T(2,128)(2,1)S(1)}, u32[]{:S(2)}, u32[]{:S(2)}) async-start(bf16[4,2,98304]{2,1,0:T(2,128)(2,1)} %reshape.118), calls=%async_computation.1 | async-start | bytes 3145728 | tf_op jit(solution)/shard_map/all_to_all | solution.py:122
  114.8 37.8 %collective-permute-start = (bf16[16,8,8,256]{3,0,2,1:T(8,128)(2,1)}, bf16[16,8,8,256]{3,0,2,1:T(8,128)(2,1)}, u32[]{:S(2)}, u32[]{:S(2)}) collective-permute-start(bf16[16,8,8,256]{3,0,2,1:T(8,128)(2,1)} %get-tuple-element.10), channel_id=1, source_target_pairs={{0,4},{4,8},{8,12},{12,16},{16,20},{20,24},{24,28},{28,0},{1,5},{5... | collective-permute-start | bytes 1572872 | tf_op jit(solution)/shard_map/ppermute | solution.py:27
  114.8 37.8 %collective-permute-start.1 = (bf16[16,8,8,256]{3,0,2,1:T(8,128)(2,1)}, bf16[16,8,8,256]{3,0,2,1:T(8,128)(2,1)}, u32[]{:S(2)}, u32[]{:S(2)}) collective-permute-start(bf16[16,8,8,256]{3,0,2,1:T(8,128)(2,1)} %get-tuple-element.11), channel_id=1, source_target_pairs={{0,28},{4,0},{8,4},{12,8},{16,12},{20,16},{24,20},{28,24},{1,29},{... | collective-permute-start | bytes 1572872 | tf_op jit(solution)/shard_map/ppermute | solution.py:27
  145.7 5.7 %copy-start.2 = (u32[32]{0:T(128)S(1)}, u32[32]{0:T(128)}, u32[]{:S(2)}) copy-start(u32[32]{0:T(128)} %constant.181) | copy-start | bytes 388
  145.7 6.9 %copy-start = (bf16[16,8,8,256]{3,0,2,1:T(8,128)(2,1)S(1)}, bf16[16,8,8,256]{3,0,2,1:T(8,128)(2,1)}, u32[]{:S(2)}) copy-start(bf16[16,8,8,256]{3,0,2,1:T(8,128)(2,1)} %get-tuple-element.12) | copy-start | bytes 1572868
  146.7 22.8 %collective-permute-start.6 = (bf16[16,8,8,256]{3,0,2,1:T(8,128)(2,1)}, bf16[16,8,8,256]{3,0,2,1:T(8,128)(2,1)S(1)}, u32[]{:S(2)}, u32[]{:S(2)}) collective-permute-start(bf16[16,8,8,256]{3,0,2,1:T(8,128)(2,1)} %get-tuple-element.7), channel_id=1, source_target_pairs={{0,4},{4,8},{8,12},{12,16},{16,20},{20,24},{24,28},{28,0},{1,5},{5... | collective-permute-start | bytes 1572872 | tf_op jit(solution)/shard_map/ppermute | solution.py:27
  146.7 25.0 %collective-permute-start.7 = (bf16[16,8,8,256]{3,0,2,1:T(8,128)(2,1)S(1)}, bf16[16,8,8,256]{3,0,2,1:T(8,128)(2,1)S(1)}, u32[]{:S(2)}, u32[]{:S(2)}) collective-permute-start(bf16[16,8,8,256]{3,0,2,1:T(8,128)(2,1)S(1)} %get-tuple-element.8), channel_id=1, source_target_pairs={{0,28},{4,0},{8,4},{12,8},{16,12},{20,16},{24,20},{28,24},{1,29},{... | collective-permute-start | bytes 1572872 | tf_op jit(solution)/shard_map/ppermute | solution.py:27
  154.8 23.5 %collective-permute-start.2 = (f32[16,48]{1,0:T(8,128)S(1)}, f32[16,48]{1,0:T(8,128)S(1)}, u32[]{:S(2)}, u32[]{:S(2)}) collective-permute-start(f32[16,48]{1,0:T(8,128)S(1)} %get-tuple-element.18), channel_id=1, source_target_pairs={{0,4},{4,8},{8,12},{12,16},{16,20},{20,24},{24,28},{28,0},{1,5},{5... | collective-permute-start | bytes 9224 | tf_op jit(solution)/shard_map/ppermute | solution.py:27
  154.8 23.4 %collective-permute-start.3 = (f32[16,48]{1,0:T(8,128)S(1)}, f32[16,48]{1,0:T(8,128)S(1)}, u32[]{:S(2)}, u32[]{:S(2)}) collective-permute-start(f32[16,48]{1,0:T(8,128)S(1)} %get-tuple-element.17), channel_id=1, source_target_pairs={{0,28},{4,0},{8,4},{12,8},{16,12},{20,16},{24,20},{28,24},{1,29},{... | collective-permute-start | bytes 9224 | tf_op jit(solution)/shard_map/ppermute | solution.py:27
  173.5 6.4 %collective-permute-start.8 = (f32[16,48]{1,0:T(8,128)S(1)}, f32[16,48]{1,0:T(8,128)S(1)}, u32[]{:S(2)}, u32[]{:S(2)}) collective-permute-start(f32[16,48]{1,0:T(8,128)S(1)} %get-tuple-element.15), channel_id=1, source_target_pairs={{0,4},{4,8},{8,12},{12,16},{16,20},{20,24},{24,28},{28,0},{1,5},{5... | collective-permute-start | bytes 9224 | tf_op jit(solution)/shard_map/ppermute | solution.py:27
  173.7 6.2 %collective-permute-start.9 = (f32[16,48]{1,0:T(8,128)S(1)}, f32[16,48]{1,0:T(8,128)S(1)}, u32[]{:S(2)}, u32[]{:S(2)}) collective-permute-start(f32[16,48]{1,0:T(8,128)S(1)} %get-tuple-element.14), channel_id=1, source_target_pairs={{0,28},{4,0},{8,4},{12,8},{16,12},{20,16},{24,20},{28,24},{1,29},{... | collective-permute-start | bytes 9224 | tf_op jit(solution)/shard_map/ppermute | solution.py:27
where the time goes:
time: 192 us; the launch traced here: 191 us
  local copies, waits for them, and re-layouts  113 us (59%)
  starting transfers between devices  33.5 us (17%)
  matrix products  15.8 us (8%)
  waiting for transfers between devices  13.7 us (7%)
  blocking collectives  10.1 us (5%)
  other arithmetic  3.34 us (2%)
    unnamed x13, local copies, waits for them, and re-layouts  56.2 us
    convert_element_type x2, local copies, waits for them, and re-layouts, place_planes(): return placed.astype(jnp.bfloat16)  24.4 us
    ppermute x8, starting transfers between devices, shifted(): return lax.ppermute(value, axis, pairs)  19 us
    all_to_all x2, local copies, waits for them, and re-layouts, local(): lax.all_to_all(frame_orbital, 'grp', split_axis=3, concat_axis=0, tiled=T...  15.1 us
    ppermute x8, waiting for transfers between devices, shifted(): return lax.ppermute(value, axis, pairs)  13.7 us
    all_to_all x2, local copies, waits for them, and re-layouts, local(): lax.all_to_all(frame_applied, 'grp', split_axis=3, concat_axis=0, tiled=T...  12.8 us
    unnamed x1, blocking collectives  10.1 us
    dot_general x1, matrix products, apply_hamiltonian(): jnp.dot(orbital.reshape(-1, cell_count), laplace_plane(), preferred_eleme...  5.15 us
  transfers between devices with their start and end apart: 12, of which 3 were waited for; matrix products, arithmetic and copies ran while one was open for 67% of the time, Pallas kernels for 0%

commit v1 on v0

v1 whole, which is shorter than its diff:
```python
import functools

import jax
import jax.numpy as jnp
import numpy as np
from jax import lax
from jax.experimental import pallas as pl
from jax.experimental.pallas import tpu as pltpu
from jax.sharding import PartitionSpec as P

COMP = 8
CX = 32
CY = 32
MESH = pl.DeviceIdType.MESH


def haar_signs():
    ids = np.arange(COMP)
    common = ids[:, None] & ids[None, :]
    parity = (common % 2 + common // 2 % 2 + common // 4 % 2) % 2
    return (1 - 2 * parity).astype(np.float32)


def matrices(members, per, seg):
    rows = members * COMP
    order = np.zeros((COMP, members, members, COMP), np.float32)
    haar = np.zeros((COMP, members, members, COMP), np.float32)
    signs = haar_signs()
    half = per // 2
    pick = np.zeros((COMP, members, members // 2, COMP), np.float32)
    for n in range(members):
        group, func = divmod(n, per)
        for c in range(COMP):
            order[c, n, n, c] = 1.0
            haar[c, n, n, :] = signs[c]
            pick[c, n, group * half + func % half, c] = 1.0
    stacked = np.concatenate([order.reshape(rows, rows), haar.reshape(rows, rows)], 0)
    lap = np.zeros((seg + 128, seg), np.float32)
    for i in range(seg):
        lap[i, i] = 3.0
        if i % CY:
            lap[i - 1, i] = -0.5
            lap[i, i - 1] = -0.5
        if i >= CY:
            lap[i - CY, i] = -0.5
            lap[i, i - CY] = -0.5
    for i in range(CY):
        lap[seg + 128 - CY + i, i] = -0.5
        lap[seg + 64 - CY + i, i] = -0.5
        lap[seg + i, seg - CY + i] = -0.5
        lap[seg + 64 + i, seg - CY + i] = -0.5
    as_bf16 = lambda value: jnp.asarray(value, jnp.bfloat16)
    return as_bf16(stacked), as_bf16(pick.reshape(rows, -1)), as_bf16(lap)


def frame_kernel(groups, depth, scal_ref, coef_ref, main_ref, halo_ref):
    per, box, comp, cells = coef_ref.shape
    seg = cells // groups
    half = per // 2
    lane = lax.broadcasted_iota(jnp.int32, (comp, 128), 1)
    for sec in range(3):
        base = scal_ref[sec]

        @pl.loop(0, depth + 2 if sec == 1 else depth + 1)
        def _(j):
            planes = []
            for f in range(per):
                p = base + j - scal_ref[3 + f]
                inside = (p >= 0) & (p < scal_ref[3 + per + f])
                value = coef_ref[f, jnp.clip(p, 0, box - 1)].astype(jnp.float32)
                planes.append(jnp.where(inside, value, 0.0))
            for g in range(groups):
                at = slice(g * seg, (g + 1) * seg)
                main_ref[sec, g, j] = jnp.concatenate([v[:, at] for v in planes], 0).astype(
                    jnp.bfloat16
                )
                tiles = []
                for v in planes:
                    zero = jnp.zeros((comp, 128), jnp.float32)
                    before = v[:, g * seg - 128 : g * seg] if g else zero
                    after = (
                        v[:, (g + 1) * seg : (g + 1) * seg + 128] if g < groups - 1 else zero
                    )
                    tiles.append(
                        jnp.where(lane >= 128 - CY, before, jnp.where(lane < CY, after, 0.0))
                    )
                packed = [
                    tiles[f] + pltpu.roll(tiles[half + f], 64, 1) for f in range(half)
                ]
                halo_ref[sec, g, j] = jnp.concatenate(packed, 0).astype(jnp.bfloat16)


def band_kernel(
    slabs,
    groups,
    depth,
    per,
    seg,
    main_ref,
    halo_ref,
    pot_ref,
    mask_ref,
    order_ref,
    pick_ref,
    lap_ref,
    margin_ref,
    ham_ref,
    got,
    got_halo,
    got_pot,
    orb,
    app,
    rows,
    got_rows,
    send_main,
    send_halo,
    send_pot,
    send_rows,
    recv_main,
    recv_halo,
    recv_pot,
    recv_rows,
):
    slab = lax.axis_index("slab")
    me = lax.axis_index("grp")
    members = groups * per
    odd = lax.rem(slab, 2)
    partner = slab + 1 - 2 * odd
    ahead = lax.rem(slab + 2, slabs)
    behind = lax.rem(slab + slabs - 2, slabs)
    frame_to = [slab, partner, lax.select(odd == 1, ahead, behind)]
    rows_to = [slab, partner, lax.select(odd == 1, behind, ahead)]
    slots = [2 * odd, 1, 2 - 2 * odd]
    shifts = [odd, 0, 1 - odd]
    counts = [depth + 1, depth + 2, depth + 1]

    @pl.loop(0, groups)
    def _(g):
        for slot in (0, 2):
            for plane in (0, depth + 1):
                got[slot, g, plane] = jnp.zeros(got.shape[3:], got.dtype)
                got_halo[slot, g, plane] = jnp.zeros(got_halo.shape[3:], got_halo.dtype)

    barrier = pltpu.get_barrier_semaphore()
    for step in range(groups):
        to = lax.rem(me + step, groups)
        for place in (slab, partner, ahead, behind):
            if place is slab and step == 0:
                continue
            pl.semaphore_signal(barrier, inc=1, device_id=(place, to), device_id_type=MESH)
    pl.semaphore_wait(barrier, 4 * groups - 1)

    def frame_copies(sec, step):
        to = lax.rem(me + step, groups)
        count, slot, shift = counts[sec], slots[sec], shifts[sec]
        out = []
        for src, dst, send, recv in (
            (main_ref, got, send_main, recv_main),
            (halo_ref, got_halo, send_halo, recv_halo),
        ):
            source = src.at[sec, to, pl.ds(0, count)]
            target = dst.at[slot, me, pl.ds(shift, count)]
            if sec == 0 and step == 0:
                out.append(pltpu.make_async_copy(source, target, recv.at[sec, me]))
            else:
                out.append(
                    pltpu.make_async_remote_copy(
                        src_ref=source,
                        dst_ref=target,
                        send_sem=send.at[sec, step],
                        recv_sem=recv.at[sec, me],
                        device_id=(frame_to[sec], to),
                        device_id_type=MESH,
                    )
                )
        return out

    pot_copy = pltpu.make_async_remote_copy(
        src_ref=pot_ref.at[:, :, pl.ds(pl.multiple_of(me * seg, seg), seg)],
        dst_ref=got_pot,
        send_sem=send_pot,
        recv_sem=recv_pot,
        device_id=(partner, me),
        device_id_type=MESH,
    )
    pot_copy.start()
    sent = []
    for step in range(groups):
        for sec in (0, 1, 2):
            for copy in frame_copies(sec, step):
                copy.start()
                if not (sec == 0 and step == 0):
                    sent.append(copy)
    pot_copy.wait_recv()

    low_lane = lax.broadcasted_iota(jnp.int32, (members * COMP, 128), 1)
    func = lax.rem(lax.broadcasted_iota(jnp.int32, (members * COMP, 128), 0), per)
    outer = (low_lane < CY) | (low_lane >= 128 - CY)
    keep = outer == (func < per // 2)

    for sec in range(3):
        slot, shift, count = slots[sec], shifts[sec], counts[sec]
        for step in range(groups):
            g = lax.rem(me + step, groups)
            for dst, recv in ((got, recv_main), (got_halo, recv_halo)):
                target = dst.at[slot, g, pl.ds(shift, count)]
                pltpu.make_async_copy(target, target, recv.at[sec, g]).wait()

        @pl.loop(0, depth + 2)
        def _(j):
            x = got[slot, :, j].reshape(members * COMP, seg)
            turned = jnp.dot(
                order_ref[: members * COMP], x, preferred_element_type=jnp.float32
            ).astype(jnp.bfloat16)
            orb[slot, j] = turned.reshape(COMP, members, seg)

        @pl.loop(0, depth)
        def _(z):
            x = got[slot, :, z + 1].reshape(members * COMP, seg)
            fine = jnp.dot(
                order_ref[members * COMP :], x, preferred_element_type=jnp.float32
            ).reshape(COMP, members, seg)
            hx = got_halo[slot, :, z + 1].reshape(members * COMP // 2, 128)
            edge = jnp.dot(pick_ref[...], hx, preferred_element_type=jnp.float32)
            edge = jnp.where(keep, edge, 0.0).astype(jnp.bfloat16)
            here = orb[slot, z + 1].reshape(members * COMP, seg)
            term = jnp.dot(here, lap_ref[:seg], preferred_element_type=jnp.float32)
            term += jnp.dot(edge, lap_ref[seg:], preferred_element_type=jnp.float32)
            term = term.reshape(COMP, members, seg)
            pot = got_pot[z].astype(jnp.float32)
            vals = [fine[k] * pot[k : k + 1] for k in range(COMP)]
            width = 1
            while width < COMP:
                vals = [
                    vals[k] + vals[k + width] if not k & width else vals[k - width] - vals[k]
                    for k in range(COMP)
                ]
                width *= 2
            inside = mask_ref[slot, z]
            inside = jnp.concatenate([inside] * (seg // 128), 1) > 0.5
            for c in range(COMP):
                beside = orb[slot, z, c].astype(jnp.float32) + orb[slot, z + 2, c].astype(
                    jnp.float32
                )
                total = term[c] - 0.5 * beside + vals[c] * (1.0 / COMP)
                app[slot, z, c] = jnp.where(inside, total, 0.0).astype(jnp.bfloat16)

    def gram(z, acc):
        for c in range(COMP):
            columns = jnp.concatenate([orb[k, z + 1, c] for k in range(3)], 0)
            images = jnp.concatenate([app[k, z, c] for k in range(3)], 0)
            acc += lax.dot_general(
                jnp.concatenate([columns, images], 0),
                columns,
                (((1,), (1,)), ((), ())),
                preferred_element_type=jnp.float32,
            )
        return acc

    wide = 3 * members
    acc = lax.fori_loop(0, depth, gram, jnp.zeros((2 * wide, wide), jnp.float32))
    rows[...] = jnp.zeros_like(rows)
    for slot in range(3):
        for g in range(groups):
            first = slot * members + g * per
            rows[slot, g, 0:per, 0:wide] = acc[first : first + per]
            rows[slot, g, per : 2 * per, 0:wide] = acc[wide + first : wide + first + per]

    for step in range(groups):
        for sec in (2, 1, 0):
            to = lax.rem(me + step, groups)
            slot = slots[sec]
            source, target = rows.at[slot, to], got_rows.at[slot, me]
            if sec == 0 and step == 0:
                copy = pltpu.make_async_copy(source, target, recv_rows.at[sec, me])
            else:
                copy = pltpu.make_async_remote_copy(
                    src_ref=source,
                    dst_ref=target,
                    send_sem=send_rows.at[sec, step],
                    recv_sem=recv_rows.at[sec, me],
                    device_id=(rows_to[sec], to),
                    device_id_type=MESH,
                )
                sent.append(copy)
            copy.start()
    for sec in range(3):
        for step in range(groups):
            g = lax.rem(me + step, groups)
            target = got_rows.at[slots[sec], g]
            pltpu.make_async_copy(target, target, recv_rows.at[sec, g]).wait()
    parts = []
    for slot in range(3):
        part = got_rows[slot, 0]
        for g in range(1, groups):
            part = part + got_rows[slot, g]
        parts.append(part)
    band = pltpu.roll(parts[0], 2 * members, 1) + pltpu.roll(parts[1], members, 1) + parts[2]
    margin_ref[...] = band[0:per, : margin_ref.shape[1]]
    ham_ref[...] = band[per : 2 * per, : ham_ref.shape[1]]
    pot_copy.wait_send()
    for copy in sent:
        copy.wait_send()


def local(slabs, groups, potential, coefficients, box_center, box_extent):
    slab = lax.axis_index("slab")
    me = lax.axis_index("grp")
    per, box, comp, cells = coefficients.shape
    depth = potential.shape[0]
    members = groups * per
    seg = cells // groups
    odd = slab % 2
    low, up = -depth, depth - 1
    bases = jnp.stack(
        [jnp.where(odd == 1, low, up), jnp.full((), -1, jnp.int32), jnp.where(odd == 1, up, low)]
    ).astype(jnp.int32)
    first = (slab * groups + me) * per
    extents = lax.dynamic_slice_in_dim(box_extent, first, per)
    centers = lax.dynamic_slice_in_dim(box_center, first, per)
    scal = jnp.concatenate([bases, centers - slab * depth - extents // 2, extents])
    vmem = pl.BlockSpec(memory_space=pltpu.VMEM)
    anywhere = pl.BlockSpec(memory_space=pl.ANY)
    main_shape = (3, groups, depth + 2, per * comp, seg)
    halo_shape = (3, groups, depth + 2, per * comp // 2, 128)
    main, halo = pl.pallas_call(
        functools.partial(frame_kernel, groups, depth),
        out_shape=(
            jax.ShapeDtypeStruct(main_shape, jnp.bfloat16),
            jax.ShapeDtypeStruct(halo_shape, jnp.bfloat16),
        ),
        in_specs=[pl.BlockSpec(memory_space=pltpu.SMEM), vmem],
        out_specs=(vmem, vmem),
        name="frames",
    )(scal, coefficients)

    owned = slab + 1 - 2 * odd
    home = (owned + jnp.arange(-1, 2) + slabs) % slabs
    ids = home[:, None] * members + jnp.arange(members)[None, :]
    begin = (
        jnp.take(box_center, ids)
        - home[:, None] * depth
        - jnp.take(box_extent, ids) // 2
        + (jnp.arange(-1, 2) * depth)[:, None]
    )
    at = jnp.arange(depth)[None, :, None] - begin[:, None, :]
    inside = (at >= 0) & (at < jnp.take(box_extent, ids)[:, None, :])
    mask = jnp.broadcast_to(
        inside.astype(jnp.float32)[..., None], (3, depth, members, 128)
    )
    order, pick, lap = matrices(members, per, seg)
    out = jax.ShapeDtypeStruct((per, 5 * members), jnp.float32)
    dma = pltpu.SemaphoreType.DMA
    return pl.pallas_call(
        functools.partial(band_kernel, slabs, groups, depth, per, seg),
        out_shape=(out, out),
        in_specs=[anywhere, anywhere, anywhere, vmem, vmem, vmem, vmem],
        out_specs=(vmem, vmem),
        scratch_shapes=[
            pltpu.VMEM(main_shape, jnp.bfloat16),
            pltpu.VMEM(halo_shape, jnp.bfloat16),
            pltpu.VMEM((depth, comp, seg), jnp.bfloat16),
            pltpu.VMEM((3, depth + 2, comp, members, seg), jnp.bfloat16),
            pltpu.VMEM((3, depth, comp, members, seg), jnp.bfloat16),
            pltpu.VMEM((3, groups, 2 * per, 128), jnp.float32),
            pltpu.VMEM((3, groups, 2 * per, 128), jnp.float32),
            dma((3, groups)),
            dma((3, groups)),
            dma,
            dma((3, groups)),
            dma((3, groups)),
            dma((3, groups)),
            dma,
            dma((3, groups)),
        ],
        compiler_params=pltpu.CompilerParams(collective_id=0, has_side_effects=True),
        name="band",
    )(main, halo, potential, mask, order, pick, lap)


def solution(mesh):
    return jax.shard_map(
        functools.partial(local, mesh.shape["slab"], mesh.shape["grp"]),
        mesh=mesh,
        in_specs=(P("slab", None, None), P(("slab", "grp"), None, None, None), P(), P()),
        out_specs=(P(("slab", "grp"), None), P(("slab", "grp"), None)),
        check_vma=False,
    )
```

time: 192 us -> 61.2 us (0.32)
  local copies, waits for them, and re-layouts: 113 us -> 6.42 us
  Pallas kernels: 0 us -> 52.9 us
  starting transfers between devices: 33.5 us -> 0 us
  matrix products: 15.8 us -> 0 us
  waiting for transfers between devices: 13.7 us -> 0 us
  blocking collectives: 10.1 us -> 0 us
  other arithmetic: 3.34 us -> 0.97 us
    unnamed x13 -> x4, local copies, waits for them, and re-layouts: 56.2 us -> 2.5 us
    pallas_call x0 -> x2, Pallas kernels: none -> 52.9 us  [the longest x1 48 us: local(): pl.pallas_call(functools.partial(band_kernel, slabs, groups, depth, per,...]
    all_to_all x4 -> x0, local copies, waits for them, and re-layouts: 27.9 us -> none  [the longest x2 15.1 us: local(): lax.all_to_all(frame_orbital, 'grp', split_axis=3, concat_axis=0, tiled=T...]
    ppermute x10 -> x0, starting transfers between devices: 25.1 us -> none  [the longest x8 19 us: shifted(): return lax.ppermute(value, axis, pairs)]
    convert_element_type x2 -> x0, local copies, waits for them, and re-layouts: 24.4 us -> none  [place_planes(): return placed.astype(jnp.bfloat16)]
    dot_general x7 -> x0, matrix products: 15.8 us -> none  [the longest x1 5.15 us: apply_hamiltonian(): jnp.dot(orbital.reshape(-1, cell_count), laplace_plane(), preferred_eleme...]
    ppermute x10 -> x0, waiting for transfers between devices: 13.7 us -> none  [the longest x8 13.7 us: shifted(): return lax.ppermute(value, axis, pairs)]
    unnamed x1 -> x0, blocking collectives: 10.1 us -> none
  transfers between devices with their start and end apart: 12 -> 0, of which waited for: 3 -> 0; matrix products, arithmetic and copies ran while one was open for 67% -> 0% of each run, Pallas kernels for 0% -> 0%
where the time goes in v1:
time: 61.2 us; the launch traced here: 61 us
  Pallas kernels  52.9 us (86%)
  local copies, waits for them, and re-layouts  6.42 us (10%)
  other arithmetic  0.97 us (2%)
  between operations  0.69 us (1%)
    pallas_call x1, Pallas kernels, local(): pl.pallas_call(functools.partial(band_kernel, slabs, groups, depth, per,...  48 us
    pallas_call x1, Pallas kernels, local(): pl.pallas_call(functools.partial(frame_kernel, groups, depth), out_shape=...  4.9 us
    unnamed x4, local copies, waits for them, and re-layouts  2.5 us
    gather x2, local copies, waits for them, and re-layouts, local(): jnp.take(box_extent, ids) // 2  1.51 us

profile of v1, /device:TPU:0, one launch (start us, length us, event | category | flops | bytes accessed | tf_op | source)
XLA Modules:
  0.0 61.0 jit_solution(18297264928332585394)
XLA Ops:
  0.6 0.0 copy-start
  0.7 0.8 %fusion.10 = (s32[4]{0:T(128)S(1)}, s32[4]{0:T(128)S(1)}) fusion(s32[128]{0:T(128)} %param.11, s32[]{:T(128)S(6)} %select_n.50, s32[]{:T(128)S(6)} %mul.37, s32[128]{0:T(128)} %param.12), kind=kLoop, calls=%fused_computation.31 | loop fusion | flops 68 | bytes 72 | tf_op jit(solution)/shard_map/sub | solution.py:321
  1.4 0.7 %concatenate.3.scal_ref = s32[11]{0:T(128)} concatenate(s32[1]{0:T(128)} %bitcast, s32[1]{0:T(128)} %constant.82.clone.1, s32[1]{0:T(128)} %bitcast.1, s32[4]{0:T(128)S(1)} %get-tuple-element.7, s32[4]{0:T(128)S(1)} %get-tuple-element.8), dimensions={0} | concatenate | bytes 88 | tf_op jit(solution)/shard_map/concatenate | solution.py:321
  2.1 0.1 compare_select_fusion
  2.2 0.1 reshape.64
  2.3 1.4 %gather_fusion.1 = s32[48]{0:T(128)S(1)} fusion(s32[128]{0:T(128)} %param.12, s32[1024]{0:T(1024)S(1)} %pad_clamp_fusion), kind=kCustom, calls=%fused_computation.1.clone | custom fusion | bytes 576 | tf_op jit(solution)/shard_map/jit(_take)/gather | solution.py:343
  3.7 0.0 copy-done
  3.7 0.8 %gather_fusion = s32[48]{0:T(128)S(1)} fusion(s32[128]{0:T(128)S(1)} %copy-done, s32[1024]{0:T(1024)S(1)} %pad_clamp_fusion), kind=kCustom, calls=%fused_computation.clone | custom fusion | bytes 576 | tf_op jit(solution)/shard_map/jit(_take)/gather | solution.py:341
  4.5 0.1 reshape.67
  4.6 0.1 reshape.71
  4.7 0.1 fusion.6
  4.8 0.8 %broadcast_in_dim.8.mask_ref = f32[3,8,16,128]{3,2,1,0:T(8,128)} broadcast(f32[3,8,16]{2,1,0:T(8,128)S(1)} %fusion.3), dimensions={0,1,2} | broadcast | bytes 198144 | tf_op jit(solution)/shard_map/broadcast_in_dim | solution.py:348
  5.6 4.9 %frames.1 = (bf16[3,4,10,32,256]{4,3,2,1,0:T(8,128)(2,1)}, bf16[3,4,10,16,128]{4,3,2,1,0:T(8,128)(2,1)}) custom-call(s32[11]{0:T(128)} %concatenate.3.scal_ref, bf16[4,16,8,1024]{3,2,1,0:T(8,128)(2,1)} %coef_ref.1), custom_call_target="tpu_custom_call" | custom-call | tf_op jit(solution)/shard_map/frames/pallas_call | solution.py:326
  10.5 48.0 %band.1 = (f32[4,80]{1,0:T(4,128)}, f32[4,80]{1,0:T(4,128)}) custom-call(bf16[3,4,10,32,256]{4,3,2,1,0:T(8,128)(2,1)} %get-tuple-element.5.main_ref, bf16[3,4,10,16,128]{4,3,2,1,0:T(8,128)(2,1)} %get-tuple-element.6.halo_ref, bf16[8,8,1024]{2,1,0:T(8,128)(2,1)} %pot_ref.1, f32[3,8,16,128]{3,2,1,0:T(8,128)} %broadcast_in_dim.8.mask_ref, ...), custom_call_target="tpu_custom_call" | custom-call | tf_op jit(solution)/shard_map/band/pallas_call | solution.py:354
  58.5 1.2 %copy.11 = f32[4,80]{1,0:T(4,128)} copy(f32[4,80]{1,0:T(4,128)} %get-tuple-element.15) | data formatting | bytes 2560
  59.7 1.3 %copy.12 = f32[4,80]{1,0:T(4,128)} copy(f32[4,80]{1,0:T(4,128)} %get-tuple-element.16) | data formatting | bytes 2560
  (4 shorter events, 0.0 us)
Async XLA Ops:
  0.6 3.1 %copy-start = (s32[128]{0:T(128)S(1)}, s32[128]{0:T(128)}, u32[]{:S(2)}) copy-start(s32[128]{0:T(128)} %param.11) | copy-start | bytes 1540

commit v2 on v1

v2 whole, which is shorter than its diff:
```python
import functools

import jax
import jax.numpy as jnp
import numpy as np
from jax import lax
from jax.experimental import pallas as pl
from jax.experimental.pallas import tpu as pltpu
from jax.sharding import PartitionSpec as P

COMP = 8
CX = 32
CY = 32
MESH = pl.DeviceIdType.MESH


def haar_signs():
    ids = np.arange(COMP)
    common = ids[:, None] & ids[None, :]
    parity = (common % 2 + common // 2 % 2 + common // 4 % 2) % 2
    return (1 - 2 * parity).astype(np.float32)


def matrices(members, per, seg):
    rows = members * COMP
    order = np.zeros((COMP, members, members, COMP), np.float32)
    haar = np.zeros((COMP, members, members, COMP), np.float32)
    signs = haar_signs()
    half = per // 2
    pick = np.zeros((COMP, members, members // 2, COMP), np.float32)
    for n in range(members):
        group, func = divmod(n, per)
        for c in range(COMP):
            order[c, n, n, c] = 1.0
            haar[c, n, n, :] = signs[c]
            pick[c, n, group * half + func % half, c] = 1.0
    stacked = np.concatenate([order.reshape(rows, rows), haar.reshape(rows, rows)], 0)
    lap = np.zeros((seg + 128, seg), np.float32)
    for i in range(seg):
        lap[i, i] = 3.0
        if i % CY:
            lap[i - 1, i] = -0.5
            lap[i, i - 1] = -0.5
        if i >= CY:
            lap[i - CY, i] = -0.5
            lap[i, i - CY] = -0.5
    for i in range(CY):
        lap[seg + 128 - CY + i, i] = -0.5
        lap[seg + 64 - CY + i, i] = -0.5
        lap[seg + i, seg - CY + i] = -0.5
        lap[seg + 64 + i, seg - CY + i] = -0.5
    as_bf16 = lambda value: jnp.asarray(value, jnp.bfloat16)
    return as_bf16(stacked), as_bf16(pick.reshape(rows, -1)), as_bf16(lap)


def band_kernel(
    slabs,
    groups,
    depth,
    coef_ref,
    pot_ref,
    center_ref,
    extent_ref,
    order_ref,
    pick_ref,
    lap_ref,
    out_ref,
    main,
    halo,
    got,
    got_halo,
    got_pot,
    orb,
    app,
    limits,
    rows,
    got_rows,
    send_main,
    send_halo,
    send_pot,
    send_rows,
    recv_main,
    recv_halo,
    recv_pot,
    recv_rows,
):
    slab = lax.axis_index("slab")
    me = lax.axis_index("grp")
    per, box, comp, cells = coef_ref.shape
    seg = cells // groups
    half = per // 2
    members = groups * per
    odd = lax.rem(slab, 2)
    partner = slab + 1 - 2 * odd
    ahead = lax.rem(slab + 2, slabs)
    behind = lax.rem(slab + slabs - 2, slabs)
    is_odd = odd == 1
    frame_to = [lax.select(is_odd, ahead, slab), partner, lax.select(is_odd, slab, behind)]
    rows_to = [lax.select(is_odd, behind, slab), partner, lax.select(is_odd, slab, ahead)]
    bases = [depth - 1, -1, -depth]
    counts = [depth, depth + 2, depth + 1]
    offsets = [0, 0, 1]
    halo_counts = [depth - 1, depth, depth]
    halo_from = [1, 1, 0]
    if groups == 4:
        targets = [lax.rem(me + 2, groups), 3 - me, me + 1 - 2 * lax.rem(me, 2), me]
    else:
        targets = [lax.rem(me + 1 + step, groups) for step in range(groups)]

    barrier = pltpu.get_barrier_semaphore()
    for to in targets:
        for place in (slab, partner, ahead, behind):
            if place is slab and to is targets[-1]:
                continue
            pl.semaphore_signal(barrier, inc=1, device_id=(place, to), device_id_type=MESH)

    @pl.loop(0, groups)
    def _(g):
        plane = jnp.zeros(got.shape[3:], got.dtype)
        got[0, g, depth] = plane
        got[0, g, depth + 1] = plane
        got[2, g, 0] = plane
        got_halo[0, g, depth - 1] = jnp.zeros(got_halo.shape[3:], got_halo.dtype)

    lane = lax.broadcasted_iota(jnp.int32, (comp, 128), 1)
    first = (slab * groups + me) * per
    extents = [extent_ref[first + f] for f in range(per)]
    starts = [
        center_ref[first + f] - slab * depth - lax.shift_right_logical(extents[f], 1)
        for f in range(per)
    ]

    def build(slot, j, with_halo):
        planes = []
        for f in range(per):
            p = bases[slot] + j - starts[f]
            inside = (p >= 0) & (p < extents[f])
            value = coef_ref[f, jnp.clip(p, 0, box - 1)].astype(jnp.float32)
            planes.append(jnp.where(inside, value, 0.0))
        for g in range(groups):
            at = slice(g * seg, (g + 1) * seg)
            main[slot, g, j] = jnp.concatenate([v[:, at] for v in planes], 0).astype(
                jnp.bfloat16
            )
            if not with_halo:
                continue
            tiles = []
            for v in planes:
                zero = jnp.zeros((comp, 128), jnp.float32)
                before = v[:, g * seg - 128 : g * seg] if g else zero
                after = v[:, (g + 1) * seg : (g + 1) * seg + 128] if g < groups - 1 else zero
                tiles.append(
                    jnp.where(lane >= 128 - CY, before, jnp.where(lane < CY, after, 0.0))
                )
            packed = [tiles[f] + pltpu.roll(tiles[half + f], 64, 1) for f in range(half)]
            halo[slot, g, j - halo_from[slot]] = jnp.concatenate(packed, 0).astype(jnp.bfloat16)

    def build_slot(slot):
        low, high = halo_from[slot], halo_from[slot] + halo_counts[slot]

        @pl.loop(low, high)
        def _(j):
            build(slot, j, True)

        for j in (*range(low), *range(high, counts[slot])):
            build(slot, j, False)

    self_slot = {0: jnp.logical_not(is_odd), 2: is_odd}
    unsent = []

    def move(slot, step, source, target, send, recv, to_slab):
        remote = pltpu.make_async_remote_copy(
            src_ref=source,
            dst_ref=target,
            send_sem=send.at[slot, step],
            recv_sem=recv.at[slot, me],
            device_id=(to_slab, targets[step]),
            device_id_type=MESH,
        )
        if slot == 1 or step < groups - 1:
            remote.start()
            unsent.append((None, remote))
            return
        here = self_slot[slot]

        @pl.when(here)
        def _():
            pltpu.make_async_copy(source, target, recv.at[slot, me]).start()

        @pl.when(jnp.logical_not(here))
        def _():
            remote.start()

        unsent.append((jnp.logical_not(here), remote))

    def send_slot(slot):
        for step, to in enumerate(targets):
            move(
                slot,
                step,
                main.at[slot, to, pl.ds(0, counts[slot])],
                got.at[slot, me, pl.ds(offsets[slot], counts[slot])],
                send_main,
                recv_main,
                frame_to[slot],
            )
            move(
                slot,
                step,
                halo.at[slot, to, pl.ds(0, halo_counts[slot])],
                got_halo.at[slot, me, pl.ds(0, halo_counts[slot])],
                send_halo,
                recv_halo,
                frame_to[slot],
            )

    pot_copy = pltpu.make_async_remote_copy(
        src_ref=pot_ref.at[:, :, pl.ds(pl.multiple_of(me * seg, seg), seg)],
        dst_ref=got_pot,
        send_sem=send_pot,
        recv_sem=recv_pot,
        device_id=(partner, me),
        device_id_type=MESH,
    )

    turn = (1, 0, 2)
    build_slot(turn[0])
    pl.semaphore_wait(barrier, 4 * groups - 1)
    build_slot(turn[1])
    send_slot(turn[0])
    pot_copy.start()
    build_slot(turn[2])
    send_slot(turn[1])

    member = lax.broadcasted_iota(jnp.int32, (members, seg), 0)
    for slot in range(3):
        home = lax.rem(partner + slot - 1 + slabs, slabs)
        begin = jnp.zeros((members, seg), jnp.int32)
        end = jnp.zeros((members, seg), jnp.int32)
        for n in range(members):
            extent = extent_ref[home * members + n]
            start = (
                center_ref[home * members + n]
                - home * depth
                - lax.shift_right_logical(extent, 1)
                + (slot - 1) * depth
            )
            begin = jnp.where(member == n, start, begin)
            end = jnp.where(member == n, start + extent, end)
        limits[slot, 0] = begin
        limits[slot, 1] = end

    send_slot(turn[2])
    pot_copy.wait_recv()

    at_lane = lax.broadcasted_iota(jnp.int32, (members * COMP, 128), 1)
    func = lax.rem(lax.broadcasted_iota(jnp.int32, (members * COMP, 128), 0), per)
    keep = ((at_lane < CY) | (at_lane >= 128 - CY)) == (func < half)

    for slot in turn:
        for g in targets[::-1]:
            for dst, recv, offset, count in (
                (got, recv_main, offsets[slot], counts[slot]),
                (got_halo, recv_halo, 0, halo_counts[slot]),
            ):
                target = dst.at[slot, g, pl.ds(offset, count)]
                pltpu.make_async_copy(target, target, recv.at[slot, g]).wait()

        @pl.loop(0, depth + 2, unroll=(depth + 2) // 2)
        def _(j):
            x = got[slot, :, j].reshape(members * COMP, seg)
            turned = jnp.dot(
                order_ref[: members * COMP], x, preferred_element_type=jnp.float32
            ).astype(jnp.bfloat16)
            orb[slot, j] = turned.reshape(COMP, members, seg)

        @pl.loop(0, depth, unroll=4)
        def _(z):
            x = got[slot, :, z + 1].reshape(members * COMP, seg)
            fine = jnp.dot(
                order_ref[members * COMP :], x, preferred_element_type=jnp.float32
            ).reshape(COMP, members, seg)
            hx = got_halo[slot, :, z].reshape(members * COMP // 2, 128)
            edge = jnp.dot(pick_ref[...], hx, preferred_element_type=jnp.float32)
            edge = jnp.where(keep, edge, 0.0).astype(jnp.bfloat16)
            here = orb[slot, z + 1].reshape(members * COMP, seg)
            term = jnp.dot(here, lap_ref[:seg], preferred_element_type=jnp.float32)
            term += jnp.dot(edge, lap_ref[seg:], preferred_element_type=jnp.float32)
            term = term.reshape(COMP, members, seg)
            pot = got_pot[z].astype(jnp.float32)
            vals = [fine[k] * pot[k : k + 1] for k in range(COMP)]
            width = 1
            while width < COMP:
                vals = [
                    vals[k] + vals[k + width] if not k & width else vals[k - width] - vals[k]
                    for k in range(COMP)
                ]
                width *= 2
            inside = (limits[slot, 0] <= z) & (limits[slot, 1] > z)
            for c in range(COMP):
                beside = orb[slot, z, c].astype(jnp.float32) + orb[slot, z + 2, c].astype(
                    jnp.float32
                )
                total = term[c] - 0.5 * beside + vals[c] * (1.0 / COMP)
                app[slot, z, c] = jnp.where(inside, total, 0.0).astype(jnp.bfloat16)

    def gram(z, acc):
        for c in range(COMP):
            columns = jnp.concatenate([orb[k, z + 1, c] for k in range(3)], 0)
            images = jnp.concatenate([app[k, z, c] for k in range(3)], 0)
            acc += lax.dot_general(
                jnp.concatenate([columns, images], 0),
                columns,
                (((1,), (1,)), ((), ())),
                preferred_element_type=jnp.float32,
            )
        return acc

    wide = 3 * members
    rows[...] = jnp.zeros_like(rows)
    acc = lax.fori_loop(0, depth, gram, jnp.zeros((2 * wide, wide), jnp.float32))
    for slot in range(3):
        for g in range(groups):
            at = slot * members + g * per
            rows[slot, g, 0:per, 0:wide] = acc[at : at + per]
            rows[slot, g, per : 2 * per, 0:wide] = acc[wide + at : wide + at + per]

    for step, to in enumerate(targets):
        for slot in (1, 0, 2):
            move(
                slot,
                step,
                rows.at[slot, to],
                got_rows.at[slot, me],
                send_rows,
                recv_rows,
                rows_to[slot],
            )
    for slot in range(3):
        for g in range(groups):
            target = got_rows.at[slot, g]
            pltpu.make_async_copy(target, target, recv_rows.at[slot, g]).wait()
    parts = []
    for slot in range(3):
        part = got_rows[slot, 0]
        for g in range(1, groups):
            part = part + got_rows[slot, g]
        parts.append(part)
    out_ref[...] = (
        pltpu.roll(parts[0], 2 * members, 1) + pltpu.roll(parts[1], members, 1) + parts[2]
    )
    pot_copy.wait_send()
    for condition, copy in unsent:
        if condition is None:
            copy.wait_send()
        else:
            pl.when(condition)(copy.wait_send)


def split_kernel(band_ref, margin_ref, ham_ref):
    per, width = margin_ref.shape
    margin_ref[...] = band_ref[:per, :width]
    ham_ref[...] = band_ref[per:, :width]


def local(slabs, groups, potential, coefficients, box_center, box_extent):
    per, box, comp, cells = coefficients.shape
    depth = potential.shape[0]
    members = groups * per
    seg = cells // groups
    vmem = pl.BlockSpec(memory_space=pltpu.VMEM)
    smem = pl.BlockSpec(memory_space=pltpu.SMEM)
    anywhere = pl.BlockSpec(memory_space=pl.ANY)
    frames = pltpu.VMEM((3, groups, depth + 2, per * comp, seg), jnp.bfloat16)
    halos = pltpu.VMEM((3, groups, depth, per * comp // 2, 128), jnp.bfloat16)
    sums = pltpu.VMEM((3, groups, 2 * per, 128), jnp.float32)
    dma = pltpu.SemaphoreType.DMA
    band = pl.pallas_call(
        functools.partial(band_kernel, slabs, groups, depth),
        out_shape=jax.ShapeDtypeStruct((2 * per, 128), jnp.float32),
        in_specs=[vmem, anywhere, smem, smem, vmem, vmem, vmem],
        out_specs=vmem,
        scratch_shapes=[
            frames,
            halos,
            frames,
            halos,
            pltpu.VMEM((depth, comp, seg), jnp.bfloat16),
            pltpu.VMEM((3, depth + 2, comp, members, seg), jnp.bfloat16),
            pltpu.VMEM((3, depth, comp, members, seg), jnp.bfloat16),
            pltpu.VMEM((3, 2, members, seg), jnp.int32),
            sums,
            sums,
            dma((3, groups)),
            dma((3, groups)),
            dma,
            dma((3, groups)),
            dma((3, groups)),
            dma((3, groups)),
            dma,
            dma((3, groups)),
        ],
        compiler_params=pltpu.CompilerParams(collective_id=0, has_side_effects=True),
        name="band",
    )(coefficients, potential, box_center, box_extent, *matrices(members, per, seg))
    out = jax.ShapeDtypeStruct((per, 5 * members), jnp.float32)
    return pl.pallas_call(
        split_kernel, out_shape=(out, out), in_specs=[vmem], out_specs=(vmem, vmem), name="split"
    )(band)


def solution(mesh):
    return jax.shard_map(
        functools.partial(local, mesh.shape["slab"], mesh.shape["grp"]),
        mesh=mesh,
        in_specs=(P("slab", None, None), P(("slab", "grp"), None, None, None), P(), P()),
        out_specs=(P(("slab", "grp"), None), P(("slab", "grp"), None)),
        check_vma=False,
    )
```

time: 61.2 us -> 44.8 us (0.73)
  Pallas kernels: 52.9 us -> 44 us
  local copies, waits for them, and re-layouts: 6.42 us -> 0 us
  other arithmetic: 0.97 us -> 0 us
    pallas_call x2, Pallas kernels: 52.9 us -> 44 us  [the longest x1 42.7 us: local(): pl.pallas_call(functools.partial(band_kernel, slabs, groups, depth), out_...]
    unnamed x4 -> x0, local copies, waits for them, and re-layouts: 2.5 us -> none
    gather x4 -> x0, local copies, waits for them, and re-layouts: 2.38 us -> none  [the longest x2 1.51 us: local(): jnp.take(box_extent, ids) // 2]
    broadcast_in_dim x2 -> x0, local copies, waits for them, and re-layouts: 0.87 us -> none  [the longest x1 0.79 us: local(): jnp.broadcast_to(inside.astype(jnp.float32)[..., None], (3, depth, member...]
    sub x1 -> x0, other arithmetic: 0.78 us -> none  [local(): centers - slab * depth - extents // 2]
    concatenate x1 -> x0, local copies, waits for them, and re-layouts: 0.67 us -> none  [local(): jnp.concatenate([bases, centers - slab * depth - extents // 2, extents])]
where the time goes in v2:
time: 44.8 us; the launch traced here: 44.6 us
  Pallas kernels  44 us (98%)
  between operations  0.64 us (1%)
    pallas_call x1, Pallas kernels, local(): pl.pallas_call(functools.partial(band_kernel, slabs, groups, depth), out_...  42.7 us
    pallas_call x1, Pallas kernels, local(): pl.pallas_call(split_kernel, out_shape=(out, out), in_specs=[vmem], out_s...  1.27 us

profile of v2, /device:TPU:0, one launch (start us, length us, event | category | flops | bytes accessed | tf_op | source)
XLA Modules:
  0.0 44.6 jit_solution(6272953811493335125)
XLA Ops:
  0.6 42.7 %band.1.band_ref = f32[8,128]{1,0:T(8,128)} custom-call(bf16[4,16,8,1024]{3,2,1,0:T(8,128)(2,1)} %coef_ref.1, bf16[8,8,1024]{2,1,0:T(8,128)(2,1)} %pot_ref.1, s32[128]{0:T(128)} %center_ref.1, s32[128]{0:T(128)} %extent_ref.1, bf16[256,128]{1,0:T(8,128)(2,1)} %constant.6.clone.order_ref, bf16[128,64]{1,0:T(8,128)(2,1)} %constant.7.clone.pick_ref, ...), custom_call_target="tpu_custom_call" | custom-call | tf_op jit(solution)/shard_map/band/pallas_call | solution.py:378
  43.3 1.3 %split.1 = (f32[4,80]{1,0:T(4,128)}, f32[4,80]{1,0:T(4,128)}) custom-call(f32[8,128]{1,0:T(8,128)} %band.1.band_ref), custom_call_target="tpu_custom_call" | custom-call | tf_op jit(solution)/shard_map/split/pallas_call | solution.py:407

commit v3 on v2

--- a/solution.py
+++ b/solution.py
@@ -95,13 +95,11 @@
     ahead = lax.rem(slab + 2, slabs)
     behind = lax.rem(slab + slabs - 2, slabs)
     is_odd = odd == 1
-    frame_to = [lax.select(is_odd, ahead, slab), partner, lax.select(is_odd, slab, behind)]
-    rows_to = [lax.select(is_odd, behind, slab), partner, lax.select(is_odd, slab, ahead)]
-    bases = [depth - 1, -1, -depth]
-    counts = [depth, depth + 2, depth + 1]
-    offsets = [0, 0, 1]
-    halo_counts = [depth - 1, depth, depth]
-    halo_from = [1, 1, 0]
+    slots = [2 * odd, 1, 2 - 2 * odd]
+    frame_to = [slab, partner, lax.select(is_odd, ahead, behind)]
+    rows_to = [slab, partner, lax.select(is_odd, behind, ahead)]
+    relayed = (0, 1) if groups == 4 else ()
+    direct = tuple(step for step in range(groups) if step not in relayed)
     if groups == 4:
         targets = [lax.rem(me + 2, groups), 3 - me, me + 1 - 2 * lax.rem(me, 2), me]
     else:
@@ -113,14 +111,6 @@
             if place is slab and to is targets[-1]:
                 continue
             pl.semaphore_signal(barrier, inc=1, device_id=(place, to), device_id_type=MESH)
-
-    @pl.loop(0, groups)
-    def _(g):
-        plane = jnp.zeros(got.shape[3:], got.dtype)
-        got[0, g, depth] = plane
-        got[0, g, depth + 1] = plane
-        got[2, g, 0] = plane
-        got_halo[0, g, depth - 1] = jnp.zeros(got_halo.shape[3:], got_halo.dtype)
 
     lane = lax.broadcasted_iota(jnp.int32, (comp, 128), 1)
     first = (slab * groups + me) * per
@@ -130,16 +120,19 @@
         for f in range(per)
     ]
 
-    def build(slot, j, with_halo):
+    def build(kind, j, with_halo):
         planes = []
         for f in range(per):
-            p = bases[slot] + j - starts[f]
+            p = j - 1 - starts[f]
+            if kind == 0:
+                p = p + depth
+                p = jnp.where(p < extents[f], p, p - 2 * depth)
             inside = (p >= 0) & (p < extents[f])
             value = coef_ref[f, jnp.clip(p, 0, box - 1)].astype(jnp.float32)
             planes.append(jnp.where(inside, value, 0.0))
         for g in range(groups):
             at = slice(g * seg, (g + 1) * seg)
-            main[slot, g, j] = jnp.concatenate([v[:, at] for v in planes], 0).astype(
+            main[kind, g, j] = jnp.concatenate([v[:, at] for v in planes], 0).astype(
                 jnp.bfloat16
             )
             if not with_halo:
@@ -153,65 +146,68 @@
                     jnp.where(lane >= 128 - CY, before, jnp.where(lane < CY, after, 0.0))
                 )
             packed = [tiles[f] + pltpu.roll(tiles[half + f], 64, 1) for f in range(half)]
-            halo[slot, g, j - halo_from[slot]] = jnp.concatenate(packed, 0).astype(jnp.bfloat16)
-
-    def build_slot(slot):
-        low, high = halo_from[slot], halo_from[slot] + halo_counts[slot]
-
-        @pl.loop(low, high)
+            halo[kind, g, j - 1] = jnp.concatenate(packed, 0).astype(jnp.bfloat16)
+
+    def build_set(kind):
+        @pl.loop(1, depth + 1)
         def _(j):
-            build(slot, j, True)
-
-        for j in (*range(low), *range(high, counts[slot])):
-            build(slot, j, False)
-
-    self_slot = {0: jnp.logical_not(is_odd), 2: is_odd}
+            build(kind, j, True)
+
+        build(kind, 0, False)
+        build(kind, depth + 1, False)
+
     unsent = []
 
-    def move(slot, step, source, target, send, recv, to_slab):
-        remote = pltpu.make_async_remote_copy(
+    def move(role, step, source, target, send, recv, to):
+        if role == 0 and step == groups - 1:
+            pltpu.make_async_copy(source, target, recv).start()
+            return
+        copy = pltpu.make_async_remote_copy(
             src_ref=source,
             dst_ref=target,
-            send_sem=send.at[slot, step],
-            recv_sem=recv.at[slot, me],
-            device_id=(to_slab, targets[step]),
+            send_sem=send.at[role, step],
+            recv_sem=recv,
+            device_id=to,
             device_id_type=MESH,
         )
-        if slot == 1 or step < groups - 1:
-            remote.start()
-            unsent.append((None, remote))
-            return
-        here = self_slot[slot]
-
-        @pl.when(here)
-        def _():
-            pltpu.make_async_copy(source, target, recv.at[slot, me]).start()
-
-        @pl.when(jnp.logical_not(here))
-        def _():
-            remote.start()
-
-        unsent.append((jnp.logical_not(here), remote))
-
-    def send_slot(slot):
-        for step, to in enumerate(targets):
+        copy.start()
+        unsent.append(copy)
+
+    def send(role, step):
+        to, kind = targets[step], role % 2
+        for source, target, sem, recv in (
+            (main, got, send_main, recv_main),
+            (halo, got_halo, send_halo, recv_halo),
+        ):
             move(
-                slot,
+                role,
                 step,
-                main.at[slot, to, pl.ds(0, counts[slot])],
-                got.at[slot, me, pl.ds(offsets[slot], counts[slot])],
-                send_main,
-                recv_main,
-                frame_to[slot],
-            )
+                source.at[kind, to],
+                target.at[role, me],
+                sem,
+                recv.at[role, me],
+                (frame_to[role], to),
+            )
+
+    def arrived(role, g):
+        for target, recv in ((got, recv_main), (got_halo, recv_halo)):
+            block = target.at[role, g]
+            pltpu.make_async_copy(block, block, recv.at[role, g]).wait()
+
+    def relay(step):
+        source = targets[step]
+        for block, sem, recv in (
+            (got, send_main, recv_main),
+            (got_halo, send_halo, recv_halo),
+        ):
             move(
-                slot,
+                2,
                 step,
-                halo.at[slot, to, pl.ds(0, halo_counts[slot])],
-                got_halo.at[slot, me, pl.ds(0, halo_counts[slot])],
-                send_halo,
-                recv_halo,
-                frame_to[slot],
+                block.at[0, source],
+                block.at[2, source],
+                sem,
+                recv.at[2, source],
+                (frame_to[2], me),
             )
 
     pot_copy = pltpu.make_async_remote_copy(
@@ -223,14 +219,16 @@
         device_id_type=MESH,
     )
 
-    turn = (1, 0, 2)
-    build_slot(turn[0])
+    build_set(0)
     pl.semaphore_wait(barrier, 4 * groups - 1)
-    build_slot(turn[1])
-    send_slot(turn[0])
+    build_set(1)
+    for step in relayed:
+        send(0, step)
+    for step in direct:
+        send(2, step)
+    for step in direct:
+        send(0, step)
     pot_copy.start()
-    build_slot(turn[2])
-    send_slot(turn[1])
 
     member = lax.broadcasted_iota(jnp.int32, (members, seg), 0)
     for slot in range(3):
@@ -250,37 +248,40 @@
         limits[slot, 0] = begin
         limits[slot, 1] = end
 
-    send_slot(turn[2])
+    for step in (*direct, *relayed):
+        send(1, step)
+    for step in relayed:
+        arrived(0, targets[step])
+        relay(step)
     pot_copy.wait_recv()
 
     at_lane = lax.broadcasted_iota(jnp.int32, (members * COMP, 128), 1)
     func = lax.rem(lax.broadcasted_iota(jnp.int32, (members * COMP, 128), 0), per)
     keep = ((at_lane < CY) | (at_lane >= 128 - CY)) == (func < half)
 
-    for slot in turn:
-        for g in targets[::-1]:
-            for dst, recv, offset, count in (
-                (got, recv_main, offsets[slot], counts[slot]),
-                (got_halo, recv_halo, 0, halo_counts[slot]),
-            ):
-                target = dst.at[slot, g, pl.ds(offset, count)]
-                pltpu.make_async_copy(target, target, recv.at[slot, g]).wait()
+    for role in range(3):
+        slot = slots[role]
+        for step in direct if role == 0 else range(groups):
+            arrived(role, targets[step])
 
         @pl.loop(0, depth + 2, unroll=(depth + 2) // 2)
         def _(j):
-            x = got[slot, :, j].reshape(members * COMP, seg)
+            x = got[role, :, j].reshape(members * COMP, seg)
             turned = jnp.dot(
                 order_ref[: members * COMP], x, preferred_element_type=jnp.float32
-            ).astype(jnp.bfloat16)
-            orb[slot, j] = turned.reshape(COMP, members, seg)
+            ).reshape(COMP, members, seg)
+            if role != 1:
+                inside = (limits[slot, 0] < j) & (limits[slot, 1] >= j)
+                turned = jnp.where(inside[None], turned, 0.0)
+            orb[slot, j] = turned.astype(jnp.bfloat16)
 
         @pl.loop(0, depth, unroll=4)
         def _(z):
-            x = got[slot, :, z + 1].reshape(members * COMP, seg)
+            x = got[role, :, z + 1].reshape(members * COMP, seg)
             fine = jnp.dot(
                 order_ref[members * COMP :], x, preferred_element_type=jnp.float32
             ).reshape(COMP, members, seg)
-            hx = got_halo[slot, :, z].reshape(members * COMP // 2, 128)
+            hx = got_halo[role, :, z].reshape(members * COMP // 2, 128)
             edge = jnp.dot(pick_ref[...], hx, preferred_element_type=jnp.float32)
             edge = jnp.where(keep, edge, 0.0).astype(jnp.bfloat16)
             here = orb[slot, z + 1].reshape(members * COMP, seg)
@@ -326,20 +327,21 @@
             rows[slot, g, per : 2 * per, 0:wide] = acc[wide + at : wide + at + per]
 
     for step, to in enumerate(targets):
-        for slot in (1, 0, 2):
+        for role in (2, 1, 0):
+            slot = slots[role]
             move(
-                slot,
+                role,
                 step,
                 rows.at[slot, to],
                 got_rows.at[slot, me],
                 send_rows,
-                recv_rows,
-                rows_to[slot],
-            )
-    for slot in range(3):
+                recv_rows.at[role, me],
+                (rows_to[role], to),
+            )
+    for role in range(3):
         for g in range(groups):
-            target = got_rows.at[slot, g]
-            pltpu.make_async_copy(target, target, recv_rows.at[slot, g]).wait()
+            block = got_rows.at[slots[role], g]
+            pltpu.make_async_copy(block, block, recv_rows.at[role, g]).wait()
     parts = []
     for slot in range(3):
         part = got_rows[slot, 0]
@@ -350,11 +352,8 @@
         pltpu.roll(parts[0], 2 * members, 1) + pltpu.roll(parts[1], members, 1) + parts[2]
     )
     pot_copy.wait_send()
-    for condition, copy in unsent:
-        if condition is None:
-            copy.wait_send()
-        else:
-            pl.when(condition)(copy.wait_send)
+    for copy in unsent:
+        copy.wait_send()
 
 
 def split_kernel(band_ref, margin_ref, ham_ref):
@@ -371,8 +370,8 @@
     vmem = pl.BlockSpec(memory_space=pltpu.VMEM)
     smem = pl.BlockSpec(memory_space=pltpu.SMEM)
     anywhere = pl.BlockSpec(memory_space=pl.ANY)
-    frames = pltpu.VMEM((3, groups, depth + 2, per * comp, seg), jnp.bfloat16)
-    halos = pltpu.VMEM((3, groups, depth, per * comp // 2, 128), jnp.bfloat16)
+    frames = lambda n: pltpu.VMEM((n, groups, depth + 2, per * comp, seg), jnp.bfloat16)
+    halos = lambda n: pltpu.VMEM((n, groups, depth, per * comp // 2, 128), jnp.bfloat16)
     sums = pltpu.VMEM((3, groups, 2 * per, 128), jnp.float32)
     dma = pltpu.SemaphoreType.DMA
     band = pl.pallas_call(
@@ -381,10 +380,10 @@
         in_specs=[vmem, anywhere, smem, smem, vmem, vmem, vmem],
         out_specs=vmem,
         scratch_shapes=[
-            frames,
-            halos,
-            frames,
-            halos,
+            frames(2),
+            halos(2),
+            frames(3),
+            halos(3),
             pltpu.VMEM((depth, comp, seg), jnp.bfloat16),
             pltpu.VMEM((3, depth + 2, comp, members, seg), jnp.bfloat16),
             pltpu.VMEM((3, depth, comp, members, seg), jnp.bfloat16),

time: 44.8 us -> 39.6 us (0.88)
  Pallas kernels: 44 us -> 38.8 us
    pallas_call x1, Pallas kernels: 42.7 us -> 37.5 us  [local(): pl.pallas_call(functools.partial(band_kernel, slabs, groups, depth), out_...]
where the time goes in v3:
time: 39.6 us; the launch traced here: 39.5 us
  Pallas kernels  38.8 us (98%)
  between operations  0.64 us (2%)
    pallas_call x1, Pallas kernels, local(): pl.pallas_call(functools.partial(band_kernel, slabs, groups, depth), out_...  37.5 us
    pallas_call x1, Pallas kernels, local(): pl.pallas_call(split_kernel, out_shape=(out, out), in_specs=[vmem], out_s...  1.27 us

profile of v3, /device:TPU:0, one launch (start us, length us, event | category | flops | bytes accessed | tf_op | source)
XLA Modules:
  0.0 39.5 jit_solution(10267527448723355007)
XLA Ops:
  0.6 37.5 %band.1.band_ref = f32[8,128]{1,0:T(8,128)} custom-call(bf16[4,16,8,1024]{3,2,1,0:T(8,128)(2,1)} %coef_ref.1, bf16[8,8,1024]{2,1,0:T(8,128)(2,1)} %pot_ref.1, s32[128]{0:T(128)} %center_ref.1, s32[128]{0:T(128)} %extent_ref.1, bf16[256,128]{1,0:T(8,128)(2,1)} %constant.6.clone.order_ref, bf16[128,64]{1,0:T(8,128)(2,1)} %constant.7.clone.pick_ref, ...), custom_call_target="tpu_custom_call" | custom-call | tf_op jit(solution)/shard_map/band/pallas_call | solution.py:377
  38.2 1.3 %split.1 = (f32[4,80]{1,0:T(4,128)}, f32[4,80]{1,0:T(4,128)}) custom-call(f32[8,128]{1,0:T(8,128)} %band.1.band_ref), custom_call_target="tpu_custom_call" | custom-call | tf_op jit(solution)/shard_map/split/pallas_call | solution.py:406

commit v4 on v3

--- a/solution.py
+++ b/solution.py
@@ -275,7 +275,7 @@
                 turned = jnp.where(inside[None], turned, 0.0)
             orb[slot, j] = turned.astype(jnp.bfloat16)
 
-        @pl.loop(0, depth, unroll=4)
+        @pl.loop(0, depth, unroll=8)
         def _(z):
             x = got[role, :, z + 1].reshape(members * COMP, seg)
             fine = jnp.dot(
@@ -319,7 +319,7 @@
 
     wide = 3 * members
     rows[...] = jnp.zeros_like(rows)
-    acc = lax.fori_loop(0, depth, gram, jnp.zeros((2 * wide, wide), jnp.float32))
+    acc = lax.fori_loop(0, depth, gram, jnp.zeros((2 * wide, wide), jnp.float32), unroll=4)
     for slot in range(3):
         for g in range(groups):
             at = slot * members + g * per

time: 39.6 us -> 38.5 us (0.972)
  Pallas kernels: 38.8 us -> 37.7 us
    pallas_call x1, Pallas kernels: 37.5 us -> 36.4 us  [local(): pl.pallas_call(functools.partial(band_kernel, slabs, groups, depth), out_...]
where the time goes in v4:
time: 38.5 us; the launch traced here: 38.3 us
  Pallas kernels  37.7 us (98%)
  between operations  0.64 us (2%)
    pallas_call x1, Pallas kernels, local(): pl.pallas_call(functools.partial(band_kernel, slabs, groups, depth), out_...  36.4 us
    pallas_call x1, Pallas kernels, local(): pl.pallas_call(split_kernel, out_shape=(out, out), in_specs=[vmem], out_s...  1.27 us

profile of v4, /device:TPU:0, one launch (start us, length us, event | category | flops | bytes accessed | tf_op | source)
XLA Modules:
  0.0 38.3 jit_solution(10147486404590187881)
XLA Ops:
  0.6 36.4 %band.1.band_ref = f32[8,128]{1,0:T(8,128)} custom-call(bf16[4,16,8,1024]{3,2,1,0:T(8,128)(2,1)} %coef_ref.1, bf16[8,8,1024]{2,1,0:T(8,128)(2,1)} %pot_ref.1, s32[128]{0:T(128)} %center_ref.1, s32[128]{0:T(128)} %extent_ref.1, bf16[256,128]{1,0:T(8,128)(2,1)} %constant.6.clone.order_ref, bf16[128,64]{1,0:T(8,128)(2,1)} %constant.7.clone.pick_ref, ...), custom_call_target="tpu_custom_call" | custom-call | tf_op jit(solution)/shard_map/band/pallas_call | solution.py:377
  37.0 1.3 %split.1 = (f32[4,80]{1,0:T(4,128)}, f32[4,80]{1,0:T(4,128)}) custom-call(f32[8,128]{1,0:T(8,128)} %band.1.band_ref), custom_call_target="tpu_custom_call" | custom-call | tf_op jit(solution)/shard_map/split/pallas_call | solution.py:406
